TPU v7x, 32 devices: a whole 2x2x4 slice. The times are simulated.
32 devices in a mesh: dp: 4 (over y, core), seq: 4 (over z), tensor: 2 (over x).
Axes of the slice: x: 2, y: 2, z: 4, core: 2. Of those that a mesh axis runs over, the one named last changes fastest.
Arguments:
- tokens: bfloat16 [8192, 2048], P(('dp', 'seq')), may hold values from -6 to 6
- out_grad: bfloat16 [8192, 2048], P(('dp', 'seq')), may hold values from -6 to 6
- positions: int32 [4, 2048], P('dp'), may hold values from 0 to 1151, as said below
- attn_gain: float32 [2048], P(('dp', 'seq')), may hold values from 0.5 to 1.5
- q_weight: float32 [2048, 2048], P(('dp', 'seq'), 'tensor'), may hold values from -0.125 to 0.125
- k_weight: float32 [2048, 512], P(('dp', 'seq'), 'tensor'), may hold values from -0.125 to 0.125
- v_weight: float32 [2048, 512], P(('dp', 'seq'), 'tensor'), may hold values from -0.125 to 0.125
- o_weight: float32 [2048, 2048], P(('dp', 'seq'), 'tensor'), may hold values from -1.5 to 1.5
- mlp_gain: float32 [2048], P(('dp', 'seq')), may hold values from 0.5 to 1.5
- gate_weight: float32 [2048, 8192], P(('dp', 'seq'), 'tensor'), may hold values from -0.125 to 0.125
- up_weight: float32 [2048, 8192], P(('dp', 'seq'), 'tensor'), may hold values from -0.125 to 0.125
- down_weight: float32 [2048, 8192], P(('dp', 'seq'), 'tensor'), may hold values from -0.0625 to 0.0625
Outputs:
- output: bfloat16 [8192, 2048], P(('dp', 'seq'))
- tokens_grad: bfloat16 [8192, 2048], P(('dp', 'seq'))
- attn_gain_grad: float32 [2048], P(('dp', 'seq'))
- q_weight_grad: float32 [2048, 2048], P(('dp', 'seq'), 'tensor')
- k_weight_grad: float32 [2048, 512], P(('dp', 'seq'), 'tensor')
- v_weight_grad: float32 [2048, 512], P(('dp', 'seq'), 'tensor')
- o_weight_grad: float32 [2048, 2048], P(('dp', 'seq'), 'tensor')
- mlp_gain_grad: float32 [2048], P(('dp', 'seq'))
- gate_weight_grad: float32 [2048, 8192], P(('dp', 'seq'), 'tensor')
- up_weight_grad: float32 [2048, 8192], P(('dp', 'seq'), 'tensor')
- down_weight_grad: float32 [2048, 8192], P(('dp', 'seq'), 'tensor')
Inputs may be any that keep to these rules, and one draw needn't show every extreme that they name: In each group, every block of 512 rows (aligned) holds 256 prompt tokens followed by 2 whole continuations of 128 rows; the prompt's positions 0 to 1023 each occur once in the group, in a drawn order; a continuation's rows hold positions 1024 to 1151 in order.
All inputs are finite; a program needn't handle non-finite values.
Results may differ from a plain program's by a relative error of at most 0.018.
Values may be sent and summed in bfloat16 or wider, within the bound.
A program may use at most 384 MiB of HBM per device.

v0:
```python
import math
import jax
import jax.numpy as jnp
import numpy as np
from jax import lax
from jax.sharding import PartitionSpec as P

HEAD_DIM = 64
PROMPT = 1024
CONT_LEN = 128
epsilon = 1e-05


def for_sending(array):
    return jax.tree.map(lambda a: a.astype(jnp.bfloat16) if a.dtype == jnp.float32 else a, array)


def rope_freqs(head_width):
    scaled_list = []
    for column in range(head_width // 2):
        inverse = 1.0 / 500000.0 ** (2.0 * column / head_width)
        wavelength = 2.0 * math.pi / inverse
        if wavelength < 2048.0:
            scaled_list.append(inverse)
        elif wavelength > 8192.0:
            scaled_list.append(inverse / 32.0)
        else:
            smooth_mix = (8192.0 / wavelength - 1.0) / 3.0
            scaled_list.append((1.0 - smooth_mix) * inverse / 32.0 + smooth_mix * inverse)
    return np.array(scaled_list, dtype=np.float32)


def rope_apply(values, cos_table, sin_table):
    half_width = values.shape[-1] // 2
    turned = jnp.concatenate([-values[..., half_width:], values[..., :half_width]], axis=-1)
    return values * cos_table + turned * sin_table


def rope_back(grads, cos_table, sin_table):
    half_width = grads.shape[-1] // 2
    twisted = grads * sin_table
    return grads * cos_table + jnp.concatenate(
        [twisted[..., half_width:], -twisted[..., :half_width]], axis=-1
    )


def norm_parts(values):
    inv_rms = lax.rsqrt(jnp.mean(values * values, axis=-1, keepdims=True) + epsilon)
    return (values * inv_rms, inv_rms)


def norm_back(grad_normed, unit_rows, inv_rms, gain_vec):
    grad_unit = grad_normed * gain_vec
    return inv_rms * (
        grad_unit - unit_rows * jnp.mean(grad_unit * unit_rows, axis=-1, keepdims=True)
    )


def times_transposed(left_side, right_side):
    return lax.dot_general(
        left_side, right_side, (((1,), (1,)), ((), ())), preferred_element_type=jnp.float32
    )


def transposed_times(left_side, right_side):
    return lax.dot_general(
        left_side, right_side, (((0,), (0,)), ((), ())), preferred_element_type=jnp.float32
    )


def local(
    tokens,
    out_grad,
    positions,
    attn_gain,
    q_weight,
    k_weight,
    v_weight,
    o_weight,
    mlp_gain,
    gate_weight,
    up_weight,
    down_weight,
):
    seq_count = lax.axis_size("seq")
    seq_rank = lax.axis_index("seq")
    tok_rows = tokens.shape[0]
    prompt_rows = PROMPT // seq_count
    cont_here = (tok_rows - prompt_rows) // CONT_LEN
    all_pos = positions[0]
    own_pos = lax.dynamic_slice_in_dim(all_pos, seq_rank * tok_rows, tok_rows)
    row_offset = jnp.arange(tok_rows, dtype=jnp.int32)
    cont_number = 1 + seq_rank * cont_here + (row_offset - prompt_rows) // CONT_LEN
    own_seg = jnp.where(row_offset < prompt_rows, jnp.zeros_like(row_offset), cont_number)
    prompt_pos = all_pos.reshape(seq_count, tok_rows)[:, :prompt_rows].reshape(-1)
    key_pos = jnp.concatenate([prompt_pos, own_pos[prompt_rows:]])
    key_seg = jnp.concatenate([jnp.zeros_like(prompt_pos), own_seg[prompt_rows:]])
    visible = (key_pos[None, :] <= own_pos[:, None]) & (
        (key_seg[None, :] == 0) | (key_seg[None, :] == own_seg[:, None])
    )
    prompt_count = prompt_pos.shape[0]
    angles = (
        own_pos.astype(jnp.float32)[:, None]
        * jnp.asarray(rope_freqs(HEAD_DIM), jnp.float32)[None, :]
    )
    angles = jnp.concatenate([angles, angles], axis=1)
    cos_table = jnp.cos(angles)[:, None, :]
    sin_table = jnp.sin(angles)[:, None, :]
    score_scale = 1.0 / math.sqrt(HEAD_DIM)

    def attn_pack():
        return (
            attn_gain.astype(jnp.bfloat16),
            q_weight.astype(jnp.bfloat16),
            k_weight.astype(jnp.bfloat16),
            v_weight.astype(jnp.bfloat16),
            o_weight.astype(jnp.bfloat16),
        )

    def mlp_pack():
        return (
            mlp_gain.astype(jnp.bfloat16),
            gate_weight.astype(jnp.bfloat16),
            up_weight.astype(jnp.bfloat16),
            down_weight.astype(jnp.bfloat16),
        )

    attn_set = lax.all_gather(for_sending(attn_pack()), ("dp", "seq"), axis=0, tiled=True)
    mlp_set = lax.all_gather(for_sending(mlp_pack()), ("dp", "seq"), axis=0, tiled=True)
    inputs = tokens.astype(jnp.float32)
    unit_one, rms_one = norm_parts(inputs)
    normed = (unit_one * attn_set[0].astype(jnp.float32)).astype(jnp.bfloat16)
    query_raw = jnp.dot(normed, attn_set[1], preferred_element_type=jnp.float32)
    key_raw = jnp.dot(normed, attn_set[2], preferred_element_type=jnp.float32)
    value_raw = jnp.dot(normed, attn_set[3], preferred_element_type=jnp.float32)
    local_heads = query_raw.shape[1] // HEAD_DIM
    local_kv = key_raw.shape[1] // HEAD_DIM
    group_size = local_heads // local_kv
    queries = rope_apply(
        query_raw.reshape(tok_rows, local_heads, HEAD_DIM), cos_table, sin_table
    ).astype(jnp.bfloat16)
    keys_own = (
        rope_apply(key_raw.reshape(tok_rows, local_kv, HEAD_DIM), cos_table, sin_table)
        .astype(jnp.bfloat16)
        .reshape(tok_rows, -1)
    )
    values_own = value_raw.astype(jnp.bfloat16)
    prompt_keys, prompt_values = (
        lax.all_gather(keys_own[:prompt_rows], "seq", axis=0, tiled=True),
        lax.all_gather(values_own[:prompt_rows], "seq", axis=0, tiled=True),
    )
    key_all = jnp.concatenate([prompt_keys, keys_own[prompt_rows:]], axis=0).reshape(
        -1, local_kv, HEAD_DIM
    )
    value_all = jnp.concatenate([prompt_values, values_own[prompt_rows:]], axis=0).reshape(
        -1, local_kv, HEAD_DIM
    )

    def head_scores(query_group, key_group):
        scores = (
            jnp.einsum("tgd,cd->gtc", query_group, key_group, preferred_element_type=jnp.float32)
            * score_scale
        )
        return jnp.where(visible[None], scores, -1e30)

    mixed_list = []
    log_totals = []
    for kv_head in range(local_kv):
        query_group = queries[:, kv_head * group_size : (kv_head + 1) * group_size, :]
        scores = head_scores(query_group, key_all[:, kv_head, :])
        row_max = jnp.max(scores, axis=-1, keepdims=True)
        exponent = jnp.exp(scores - row_max)
        row_total = jnp.sum(exponent, axis=-1, keepdims=True)
        probability = exponent / row_total
        log_totals.append(row_max + jnp.log(row_total))
        mixed_list.append(
            jnp.einsum(
                "gtc,cd->tgd",
                probability.astype(jnp.bfloat16),
                value_all[:, kv_head, :],
                preferred_element_type=jnp.float32,
            )
        )
    attended = jnp.concatenate(mixed_list, axis=1).reshape(tok_rows, -1).astype(jnp.bfloat16)
    middle = inputs + lax.psum(
        times_transposed(attended, attn_set[4]).astype(jnp.bfloat16), "tensor"
    ).astype(jnp.float32)
    unit_two, rms_two = norm_parts(middle)
    normed_two = (unit_two * mlp_set[0].astype(jnp.float32)).astype(jnp.bfloat16)
    gate_pre = jnp.dot(normed_two, mlp_set[1], preferred_element_type=jnp.float32)
    upward = jnp.dot(normed_two, mlp_set[2], preferred_element_type=jnp.float32)
    sigmoid_gate = jax.nn.sigmoid(gate_pre)
    activated = gate_pre * sigmoid_gate
    hidden = (activated * upward).astype(jnp.bfloat16)
    result = middle + lax.psum(
        times_transposed(hidden, mlp_set[3]).astype(jnp.bfloat16), "tensor"
    ).astype(jnp.float32)
    output = result.astype(jnp.bfloat16)
    grad_out = out_grad.astype(jnp.float32)
    grad_hidden = jnp.dot(out_grad, mlp_set[3], preferred_element_type=jnp.float32)
    grad_gate = (
        grad_hidden * upward * sigmoid_gate * (1.0 + gate_pre * (1.0 - sigmoid_gate))
    ).astype(jnp.bfloat16)
    grad_up = (grad_hidden * activated).astype(jnp.bfloat16)
    grad_normed_two = lax.psum(
        (times_transposed(grad_gate, mlp_set[1]) + times_transposed(grad_up, mlp_set[2])).astype(
            jnp.bfloat16
        ),
        "tensor",
    ).astype(jnp.float32)
    gain_two_grad = jnp.sum(grad_normed_two * unit_two, axis=0)
    grad_middle = grad_out + norm_back(
        grad_normed_two, unit_two, rms_two, mlp_set[0].astype(jnp.float32)
    )

    def summed(term):
        return lax.psum_scatter(
            term.astype(jnp.bfloat16), ("dp", "seq"), scatter_dimension=0, tiled=True
        ).astype(jnp.float32)

    down_grad = summed(transposed_times(out_grad, hidden))
    gate_grad = summed(transposed_times(normed_two, grad_gate))
    up_grad = summed(transposed_times(normed_two, grad_up))
    grad_branch = grad_middle.astype(jnp.bfloat16)
    grad_attended = (
        jnp.dot(grad_branch, attn_set[4], preferred_element_type=jnp.float32)
        .astype(jnp.bfloat16)
        .reshape(tok_rows, local_heads, HEAD_DIM)
    )
    query_grads = []
    key_grads = []
    value_grads = []
    for kv_head in range(local_kv):
        query_group = queries[:, kv_head * group_size : (kv_head + 1) * group_size, :]
        key_group = key_all[:, kv_head, :]
        value_group = value_all[:, kv_head, :]
        grad_group = grad_attended[:, kv_head * group_size : (kv_head + 1) * group_size, :]
        probability = jnp.exp(head_scores(query_group, key_group) - log_totals[kv_head])
        grad_prob = jnp.einsum(
            "tgd,cd->gtc", grad_group, value_group, preferred_element_type=jnp.float32
        )
        row_dot = jnp.sum(probability * grad_prob, axis=-1, keepdims=True)
        grad_scores = (probability * (grad_prob - row_dot)).astype(jnp.bfloat16)
        query_grads.append(
            jnp.einsum("gtc,cd->tgd", grad_scores, key_group, preferred_element_type=jnp.float32)
            * score_scale
        )
        key_grads.append(
            jnp.einsum("gtc,tgd->cd", grad_scores, query_group, preferred_element_type=jnp.float32)
            * score_scale
        )
        value_grads.append(
            jnp.einsum(
                "gtc,tgd->cd",
                probability.astype(jnp.bfloat16),
                grad_group,
                preferred_element_type=jnp.float32,
            )
        )
    grad_queries = jnp.concatenate(query_grads, axis=1)
    grad_keys = jnp.stack(key_grads, axis=1).reshape(-1, local_kv * HEAD_DIM)
    grad_values = jnp.stack(value_grads, axis=1).reshape(-1, local_kv * HEAD_DIM)
    key_share, value_share = (
        lax.psum_scatter(
            grad_keys[:prompt_count].astype(jnp.bfloat16), "seq", scatter_dimension=0, tiled=True
        ).astype(jnp.float32),
        lax.psum_scatter(
            grad_values[:prompt_count].astype(jnp.bfloat16), "seq", scatter_dimension=0, tiled=True
        ).astype(jnp.float32),
    )
    grad_key_own = jnp.concatenate([key_share, grad_keys[prompt_count:]], axis=0).reshape(
        tok_rows, local_kv, HEAD_DIM
    )
    grad_query_raw = (
        rope_back(grad_queries, cos_table, sin_table).reshape(tok_rows, -1).astype(jnp.bfloat16)
    )
    grad_key_raw = (
        rope_back(grad_key_own, cos_table, sin_table).reshape(tok_rows, -1).astype(jnp.bfloat16)
    )
    grad_value_raw = jnp.concatenate([value_share, grad_values[prompt_count:]], axis=0).astype(
        jnp.bfloat16
    )
    grad_normed = lax.psum(
        (
            times_transposed(grad_query_raw, attn_set[1])
            + times_transposed(grad_key_raw, attn_set[2])
            + times_transposed(grad_value_raw, attn_set[3])
        ).astype(jnp.bfloat16),
        "tensor",
    ).astype(jnp.float32)
    gain_one_grad = jnp.sum(grad_normed * unit_one, axis=0)
    grad_inputs = grad_middle + norm_back(
        grad_normed, unit_one, rms_one, attn_set[0].astype(jnp.float32)
    )
    attn_terms = (
        gain_one_grad,
        transposed_times(normed, grad_query_raw),
        transposed_times(normed, grad_key_raw),
        transposed_times(normed, grad_value_raw),
        transposed_times(grad_branch, attended),
        gain_two_grad,
    )
    attn_grads = (
        lax.psum_scatter(attn_terms[0], ("dp", "seq"), scatter_dimension=0, tiled=True),
        summed(attn_terms[1]),
        summed(attn_terms[2]),
        summed(attn_terms[3]),
        summed(attn_terms[4]),
        lax.psum_scatter(attn_terms[5], ("dp", "seq"), scatter_dimension=0, tiled=True),
    )
    return (
        output,
        grad_inputs.astype(jnp.bfloat16),
        attn_grads[0],
        attn_grads[1],
        attn_grads[2],
        attn_grads[3],
        attn_grads[4],
        attn_grads[5],
        gate_grad,
        up_grad,
        down_grad,
    )


def solution(mesh):
    placed = (
        P(("dp", "seq"), None),
        P(("dp", "seq"), None),
        P("dp", None),
        P(("dp", "seq")),
        P(("dp", "seq"), "tensor"),
        P(("dp", "seq"), "tensor"),
        P(("dp", "seq"), "tensor"),
        P(("dp", "seq"), "tensor"),
        P(("dp", "seq")),
        P(("dp", "seq"), "tensor"),
        P(("dp", "seq"), "tensor"),
        P(("dp", "seq"), "tensor"),
    )
    return jax.shard_map(
        local,
        mesh=mesh,
        in_specs=placed,
        out_specs=(
            P(("dp", "seq"), None),
            P(("dp", "seq"), None),
            P(("dp", "seq")),
            P(("dp", "seq"), "tensor"),
            P(("dp", "seq"), "tensor"),
            P(("dp", "seq"), "tensor"),
            P(("dp", "seq"), "tensor"),
            P(("dp", "seq")),
            P(("dp", "seq"), "tensor"),
            P(("dp", "seq"), "tensor"),
            P(("dp", "seq"), "tensor"),
        ),
        check_vma=False,
    )
```

profile of v0, /device:TPU:0, one launch (start us, length us, event | category | flops | bytes accessed | tf_op | source)
XLA Modules:
  0.0 1811.2 jit_solution(7538030029307712680)
XLA Ops:
  18.5 33.9 %all-gather = bf16[16,1,128]{2,1,0:T(2,128)(2,1)S(1)} all-gather(bf16[1,1,128]{2,1,0:T(2,128)(2,1)S(1)} %convert_bitcast_fusion.2), channel_id=1, replica_groups=mesh['dp'=4,'seq'=4,'tensor'=2] {'dp','seq'}, dimensions={0}, use_global_device_ids=true | all-gather | bytes 4352 | tf_op jit(solution)/shard_map/all_gather | solution.py:128
  57.3 15.7 all_gather.35
  76.1 15.8 all-gather.12.cloned.1.call-done
  94.3 19.1 %all_gather.37 = bf16[1024,256]{0,1:T(8,128)(2,1)S(1)} all-gather(bf16[256,256]{0,1:T(8,128)(2,1)S(1)} %bitcast.279), channel_id=1, replica_groups=mesh['dp'=4,'seq'=4,'tensor'=2] {'seq'}, dimensions={0}, use_global_device_ids=true | all-gather | bytes 655360 | tf_op jit(solution)/shard_map/all_gather | solution.py:149
  114.1 31.9 %all-gather.14.cloned.1.call-done = bf16[2048,1024]{1,0:T(8,128)(2,1)} async-done(((bf16[128,1024]{1,0:T(8,128)(2,1)}), bf16[2048,1024]{1,0:T(8,128)(2,1)}) %all-gather.14.cloned.1.call-update) | async-done | bytes 4194320 | tf_op jit(solution)/shard_map/all_gather | solution.py:128
  212.9 31.2 %all-gather.1 = bf16[16,1,128]{2,1,0:T(2,128)(2,1)S(1)} all-gather(bf16[1,1,128]{2,1,0:T(2,128)(2,1)S(1)} %convert_bitcast_fusion.1), channel_id=1, replica_groups=mesh['dp'=4,'seq'=4,'tensor'=2] {'dp','seq'}, dimensions={0}, use_global_device_ids=true | all-gather | bytes 4352 | tf_op jit(solution)/shard_map/all_gather | solution.py:129
  246.6 20.1 %all-reduce.9.cloned.1.call-done = bf16[512,2048]{1,0:T(8,128)(2,1)} async-done(((bf16[512,2048]{1,0:T(8,128)(2,1)}), bf16[512,2048]{1,0:T(8,128)(2,1)}) %all-reduce.9.cloned.1.call-update) | async-done | bytes 2097168 | tf_op jit(solution)/shard_map/psum | solution.py:185
  271.6 124.2 %all-gather.20.cloned.1.call-done = bf16[2048,4096]{1,0:T(8,128)(2,1)} async-done(((bf16[128,4096]{1,0:T(8,128)(2,1)}), bf16[2048,4096]{1,0:T(8,128)(2,1)}) %all-gather.20.cloned.1.call-update) | async-done | bytes 16777232 | tf_op jit(solution)/shard_map/all_gather | solution.py:129
  395.8 15.2 fusion.159
  411.0 112.2 %all-gather.18.cloned.1.call-done = bf16[2048,4096]{1,0:T(8,128)(2,1)} async-done(((bf16[128,4096]{1,0:T(8,128)(2,1)}), bf16[2048,4096]{1,0:T(8,128)(2,1)}) %all-gather.18.cloned.1.call-update) | async-done | bytes 16777232 | tf_op jit(solution)/shard_map/all_gather | solution.py:129
  523.2 15.1 fusion.158
  538.3 112.4 %all-gather.22.cloned.1.call-done = bf16[2048,4096]{1,0:T(8,128)(2,1)} async-done(((bf16[128,4096]{1,0:T(8,128)(2,1)}), bf16[2048,4096]{1,0:T(8,128)(2,1)}) %all-gather.22.cloned.1.call-update) | async-done | bytes 16777232 | tf_op jit(solution)/shard_map/all_gather | solution.py:129
  650.6 22.2 %multiply_convert_fusion = (bf16[512,4096]{1,0:T(8,128)(2,1)}, bf16[512,4096]{1,0:T(8,128)(2,1)}, bf16[512,4096]{1,0:T(8,128)(2,1)}) fusion(f32[512,4096]{1,0:T(8,128)} %fusion.158, f32[512,4096]{1,0:T(8,128)} %fusion.159, bf16[512,2048]{1,0:T(8,128)(2,1)} %param.14, bf16[2048,4096]{1,0:T(8,128)(2,1)} %all-gather.22.cloned.1.call-done), kind=kOutput, calls=%fused_computation.43 | convolution fusion | flops 8621391872 | bytes 48234496 | tf_op jit(solution)/shard_map/dot_general | solution.py:200
  672.8 15.4 fusion.160
  702.5 15.7 convolution_convert_fusion.5
  718.3 45.5 %all-reduce.11.cloned.1.call-done = bf16[512,2048]{1,0:T(8,128)(2,1)} async-done(((bf16[512,2048]{1,0:T(8,128)(2,1)}), bf16[512,2048]{1,0:T(8,128)(2,1)}) %all-reduce.11.cloned.1.call-update) | async-done | bytes 2097168 | tf_op jit(solution)/shard_map/psum | solution.py:205
  923.8 21.0 %copy.109 = bf16[2048,4096]{1,0:T(8,128)(2,1)} copy(bf16[2048,4096]{0,1:T(8,128)(2,1)} %convert_bitcast_fusion) | data formatting | bytes 33554432
  978.6 19.4 %reduce-scatter.18.cloned.1.call-done = bf16[128,256]{1,0:T(8,128)(2,1)} async-done(((bf16[2048,256]{1,0:T(8,128)(2,1)}), bf16[128,256]{1,0:T(8,128)(2,1)}) %reduce-scatter.18.cloned.1.call-update) | async-done | bytes 65552 | tf_op jit(solution)/shard_map/reduce_scatter | solution.py:217
  999.5 108.4 %all-reduce.13.cloned.1.call-done = (bf16[512,2048]{1,0:T(8,128)(2,1)}, bf16[512,2048]{1,0:T(8,128)(2,1)}) async-done(((bf16[512,2048]{1,0:T(8,128)(2,1)}, bf16[512,2048]{1,0:T(8,128)(2,1)}), (bf16[512,2048]{1,0:T(8,128)(2,1)}, bf16[512,2048]{1,0:T(8,128)(2,1)})) %all-reduce.13.cloned.1.call-update) | async-done | bytes 4194320 | tf_op jit(solution)/shard_map/psum | solution.py:195
  1110.8 62.4 %all-reduce.3 = (f32[2048]{0:T(1024)S(1)}, f32[2048]{0:T(1024)S(1)}) all-reduce(f32[2048]{0:T(1024)S(1)} %get-tuple-element.46, f32[2048]{0:T(1024)S(1)} %copy-done.54), channel_id=4, replica_groups=mesh['dp'=4,'seq'=4,'tensor'=2] {'dp','seq'}, use_global_device_ids=true, to_apply=%region_23.24.clone | all-reduce | flops 4096 | bytes 32768
  1186.4 73.8 %reduce-scatter.16.cloned.1.call-done = bf16[128,1024]{1,0:T(8,128)(2,1)} async-done(((bf16[2048,1024]{1,0:T(8,128)(2,1)}), bf16[128,1024]{1,0:T(8,128)(2,1)}) %reduce-scatter.16.cloned.1.call-update) | async-done | bytes 262160 | tf_op jit(solution)/shard_map/reduce_scatter | solution.py:217
  1262.0 178.6 %reduce-scatter.28.cloned.1.call-done = bf16[128,4096]{1,0:T(8,128)(2,1)} async-done(((bf16[2048,4096]{1,0:T(8,128)(2,1)}), bf16[128,4096]{1,0:T(8,128)(2,1)}) %reduce-scatter.28.cloned.1.call-update) | async-done | bytes 1048592
  1443.9 177.2 %reduce-scatter.26.cloned.1.call-done = bf16[128,4096]{1,0:T(8,128)(2,1)} async-done(((bf16[2048,4096]{1,0:T(8,128)(2,1)}), bf16[128,4096]{1,0:T(8,128)(2,1)}) %reduce-scatter.26.cloned.1.call-update) | async-done | bytes 1048592 | tf_op jit(solution)/shard_map/reduce_scatter | solution.py:217
  1623.8 177.8 %reduce-scatter.24.cloned.1.call-done = bf16[128,4096]{1,0:T(8,128)(2,1)} async-done(((bf16[2048,4096]{1,0:T(8,128)(2,1)}), bf16[128,4096]{1,0:T(8,128)(2,1)}) %reduce-scatter.24.cloned.1.call-update) | async-done | bytes 1048592 | tf_op jit(solution)/shard_map/reduce_scatter | solution.py:217
  (341 shorter events, 330.8 us)
Async XLA Ops:
  7.2 48.1 %all-gather.10.cloned.1.call-start = ((), (), s32[]{:S(2)}) async-start(), calls=%async_computation.9 | async-start | bytes 1114112 | tf_op jit(solution)/shard_map/all_gather | solution.py:128
  9.0 82.9 %all-gather.12.cloned.1.call-start = ((), (), s32[]{:S(2)}) async-start(), calls=%async_computation.10 | async-start | bytes 1114112 | tf_op jit(solution)/shard_map/all_gather | solution.py:128
  10.6 135.3 %all-gather.14.cloned.1.call-start = ((), (), s32[]{:S(2)}) async-start(), calls=%async_computation.11 | async-start | bytes 4456448 | tf_op jit(solution)/shard_map/all_gather | solution.py:128
  12.4 185.8 %all-gather.16.cloned.1.call-start = ((), (), s32[]{:S(2)}) async-start(), calls=%async_computation.12 | async-start | bytes 4456448 | tf_op jit(solution)/shard_map/all_gather | solution.py:128
  14.3 252.4 %all-reduce.9.cloned.1.call-start = ((), (), s32[]{:S(2)}) async-start(), calls=%async_computation.13 | async-start | bytes 4194304 | tf_op jit(solution)/shard_map/psum | solution.py:185
  18.5 127.4 %copy-start.55 = (f32[512]{0:T(512)}, f32[512]{0:T(512)S(1)}, u32[]{:S(2)}) copy-start(f32[512]{0:T(512)S(1)} %add_rsqrt_fusion.1) | copy-start | bytes 6148
  52.4 93.5 %copy-start.52 = (f32[16,1,128]{2,1,0:T(1,128)}, f32[16,1,128]{2,1,0:T(1,128)S(1)}, u32[]{:S(2)}) copy-start(f32[16,1,128]{2,1,0:T(1,128)S(1)} %convert_element_type.283) | copy-start | bytes 24580
  54.0 96.8 %copy-start.16 = (f32[512,64]{0,1:T(8,128)}, f32[512,64]{0,1:T(8,128)S(1)}, u32[]{:S(2)}) copy-start(f32[512,64]{0,1:T(8,128)S(1)} %get-tuple-element.70) | copy-start | bytes 393220
  94.3 73.3 %copy-start.10 = (bf16[256,4,64]{0,2,1:T(8,128)(2,1)}, bf16[256,4,64]{0,2,1:T(8,128)(2,1)S(1)}, u32[]{:S(2)}) copy-start(bf16[256,4,64]{0,2,1:T(8,128)(2,1)S(1)} %get-tuple-element.68) | copy-start | bytes 393220
  204.5 191.3 %all-gather.20.cloned.1.call-start = ((), (), s32[]{:S(2)}) async-start(), calls=%async_computation.15 | async-start | bytes 17825792 | tf_op jit(solution)/shard_map/all_gather | solution.py:129
  207.3 315.9 %all-gather.18.cloned.1.call-start = ((), (), s32[]{:S(2)}) async-start(), calls=%async_computation.14 | async-start | bytes 17825792 | tf_op jit(solution)/shard_map/all_gather | solution.py:129
  210.1 440.6 %all-gather.22.cloned.1.call-start = ((), (), s32[]{:S(2)}) async-start(), calls=%async_computation.16 | async-start | bytes 17825792 | tf_op jit(solution)/shard_map/all_gather | solution.py:129
  212.8 550.9 %all-reduce.11.cloned.1.call-start = ((), (), s32[]{:S(2)}) async-start(), calls=%async_computation.17 | async-start | bytes 4194304 | tf_op jit(solution)/shard_map/psum | solution.py:205
  702.5 162.0 %reduce-scatter.14.cloned.1.call-start = ((), (), s32[]{:S(2)}) async-start(), calls=%async_computation.19 | async-start | bytes 655360 | tf_op jit(solution)/shard_map/reduce_scatter | solution.py:267
  811.7 65.9 %reduce-scatter.12.cloned.1.call-start = ((), (), s32[]{:S(2)}) async-start(), calls=%async_computation.18 | async-start | bytes 655360 | tf_op jit(solution)/shard_map/reduce_scatter | solution.py:264
  855.7 121.4 %reduce-scatter.20.cloned.1.call-start = ((), (), s32[]{:S(2)}) async-start(), calls=%async_computation.22 | async-start | bytes 1114112 | tf_op jit(solution)/shard_map/reduce_scatter | solution.py:217
  867.5 130.4 %reduce-scatter.18.cloned.1.call-start = ((), (), s32[]{:S(2)}) async-start(), calls=%async_computation.21 | async-start | bytes 1114112 | tf_op jit(solution)/shard_map/reduce_scatter | solution.py:217
  883.4 224.5 %all-reduce.13.cloned.1.call-start = ((), (), s32[]{:S(2)}) async-start(), calls=%async_computation.27 | async-start | bytes 8388608 | tf_op jit(solution)/shard_map/psum | solution.py:195
  892.9 291.8 %reduce-scatter.22.cloned.1.call-start = ((), (), s32[]{:S(2)}) async-start(), calls=%async_computation.23 | async-start | bytes 4456448 | tf_op jit(solution)/shard_map/reduce_scatter | solution.py:217
  902.9 357.3 %reduce-scatter.16.cloned.1.call-start = ((), (), s32[]{:S(2)}) async-start(), calls=%async_computation.20 | async-start | bytes 4456448 | tf_op jit(solution)/shard_map/reduce_scatter | solution.py:217
  908.8 531.9 %reduce-scatter.28.cloned.1.call-start = ((), (), s32[]{:S(2)}) async-start(), calls=%async_computation.26 | async-start | bytes 17825792
  944.8 676.3 %reduce-scatter.26.cloned.1.call-start = ((), (), s32[]{:S(2)}) async-start(), calls=%async_computation.25 | async-start | bytes 17825792 | tf_op jit(solution)/shard_map/reduce_scatter | solution.py:217
  959.9 841.8 %reduce-scatter.24.cloned.1.call-start = ((), (), s32[]{:S(2)}) async-start(), calls=%async_computation.24 | async-start | bytes 17825792 | tf_op jit(solution)/shard_map/reduce_scatter | solution.py:217
  975.2 135.6 %copy-start.54 = (f32[2048]{0:T(1024)S(1)}, f32[2048]{0:T(1024)}, u32[]{:S(2)}) copy-start(f32[2048]{0:T(1024)} %get-tuple-element.44) | copy-start | bytes 24580
  (78 other events, 781.5 us)
Sparse Core Ops, SparseCore 0:
  10.8 40.5 all-gather.9
  54.2 37.6 all-gather.11
  94.7 51.2 all-gather.13
  148.6 48.8 all-gather.15
  204.6 62.0 all-reduce.8
  269.3 126.4 all-gather.19
  398.6 124.5 all-gather.17
  526.0 124.5 all-gather.21
  702.6 61.1 all-reduce.10
  811.9 21.8 reduce-scatter.13
  855.8 21.7 reduce-scatter.11
  881.1 55.9 reduce-scatter.19
  941.2 56.6 reduce-scatter.17
  1000.9 106.9 all-reduce.12
  1111.6 72.9 reduce-scatter.21
  1188.3 71.8 reduce-scatter.15
  1264.2 176.4 reduce-scatter.27
  1444.6 176.4 reduce-scatter.25
  1625.2 176.4 reduce-scatter.23
where the time goes:
time: 1820 us; the launch traced here: 1810 us
  waiting for transfers between devices  1200 us (66%)
  matrix products  270 us (15%)
  blocking collectives  162 us (9%)
  other arithmetic  112 us (6%)
  local copies, waits for them, and re-layouts  44.3 us (2%)
    reduce_scatter x6, waiting for transfers between devices, summed(): lax.psum_scatter(term.astype(jnp.bfloat16), ('dp', 'seq'), scatter_dimens...  450 us
    all_gather x3, waiting for transfers between devices, local(): lax.all_gather(for_sending(mlp_pack()), ('dp', 'seq'), axis=0, tiled=True)  349 us
    unnamed x20, waiting for transfers between devices  179 us
    psum x1, waiting for transfers between devices, local(): lax.psum(times_transposed(hidden, mlp_set[3]).astype(jnp.bfloat16), 'tens...  108 us
    dot_general x7, matrix products, transposed_times(): lax.dot_general(left_side, right_side, (((0,), (0,)), ((), ())), preferre...  63.4 us
    unnamed x1, blocking collectives  62.4 us
    dot_general x7, matrix products, times_transposed(): lax.dot_general(left_side, right_side, (((1,), (1,)), ((), ())), preferre...  56.9 us
    all_gather x4, waiting for transfers between devices, local(): lax.all_gather(for_sending(attn_pack()), ('dp', 'seq'), axis=0, tiled=True)  47.7 us
  transfers between devices with their start and end apart: 19, of which 15 were waited for; matrix products, arithmetic and copies ran while one was open for 17% of the time, Pallas kernels for 0%

commit v1 on v0

--- a/solution.py
+++ b/solution.py
@@ -202,11 +202,14 @@
         grad_hidden * upward * sigmoid_gate * (1.0 + gate_pre * (1.0 - sigmoid_gate))
     ).astype(jnp.bfloat16)
     grad_up = (grad_hidden * activated).astype(jnp.bfloat16)
-    grad_normed_two = lax.psum(
-        (times_transposed(grad_gate, mlp_set[1]) + times_transposed(grad_up, mlp_set[2])).astype(
-            jnp.bfloat16
+    grad_normed_two = jnp.sum(
+        lax.all_gather(
+            (
+                times_transposed(grad_gate, mlp_set[1]) + times_transposed(grad_up, mlp_set[2])
+            ).astype(jnp.bfloat16),
+            "tensor",
         ),
-        "tensor",
+        axis=0,
     ).astype(jnp.float32)
     gain_two_grad = jnp.sum(grad_normed_two * unit_two, axis=0)
     grad_middle = grad_out + norm_back(

time: 1820 us -> 1820 us (level)
    psum x1 -> x0, waiting for transfers between devices: 45.5 us -> none  [local(): lax.psum((times_transposed(grad_gate, mlp_set[1]) + times_transposed(grad...]
    all_gather x0 -> x1, waiting for transfers between devices: none -> 39.4 us  [local(): lax.all_gather((times_transposed(grad_gate, mlp_set[1]) + times_transpose...]
    unnamed x175 -> x183, local copies, waits for them, and re-layouts: 37.5 us -> 37.6 us
where the time goes in v1:
time: 1820 us; the launch traced here: 1810 us
  waiting for transfers between devices  1200 us (66%)
  matrix products  270 us (15%)
  blocking collectives  162 us (9%)
  other arithmetic  115 us (6%)
  local copies, waits for them, and re-layouts  44.4 us (2%)
    reduce_scatter x6, waiting for transfers between devices, summed(): lax.psum_scatter(term.astype(jnp.bfloat16), ('dp', 'seq'), scatter_dimens...  450 us
    all_gather x3, waiting for transfers between devices, local(): lax.all_gather(for_sending(mlp_pack()), ('dp', 'seq'), axis=0, tiled=True)  349 us
    unnamed x20, waiting for transfers between devices  179 us
    psum x1, waiting for transfers between devices, local(): lax.psum(times_transposed(hidden, mlp_set[3]).astype(jnp.bfloat16), 'tens...  109 us
    dot_general x7, matrix products, transposed_times(): lax.dot_general(left_side, right_side, (((0,), (0,)), ((), ())), preferre...  63.4 us
    unnamed x1, blocking collectives  62.4 us
    dot_general x7, matrix products, times_transposed(): lax.dot_general(left_side, right_side, (((1,), (1,)), ((), ())), preferre...  56.6 us
    all_gather x4, waiting for transfers between devices, local(): lax.all_gather(for_sending(attn_pack()), ('dp', 'seq'), axis=0, tiled=True)  47.7 us
  transfers between devices with their start and end apart: 19, of which 15 were waited for; matrix products, arithmetic and copies ran while one was open for 17% of the time, Pallas kernels for 0%

profile of v1, /device:TPU:0, one launch (start us, length us, event | category | flops | bytes accessed | tf_op | source)
XLA Modules:
  0.0 1810.0 jit_solution(14175947568555046593)
XLA Ops:
  18.5 33.9 %all-gather.1 = bf16[16,1,128]{2,1,0:T(2,128)(2,1)S(1)} all-gather(bf16[1,1,128]{2,1,0:T(2,128)(2,1)S(1)} %convert_bitcast_fusion.2), channel_id=1, replica_groups=mesh['dp'=4,'seq'=4,'tensor'=2] {'dp','seq'}, dimensions={0}, use_global_device_ids=true | all-gather | bytes 4352 | tf_op jit(solution)/shard_map/all_gather | solution.py:128
  57.3 15.7 all_gather.41
  76.1 15.8 all-gather.14.cloned.1.call-done
  94.3 19.1 %all_gather.43 = bf16[1024,256]{0,1:T(8,128)(2,1)S(1)} all-gather(bf16[256,256]{0,1:T(8,128)(2,1)S(1)} %bitcast.281), channel_id=1, replica_groups=mesh['dp'=4,'seq'=4,'tensor'=2] {'seq'}, dimensions={0}, use_global_device_ids=true | all-gather | bytes 655360 | tf_op jit(solution)/shard_map/all_gather | solution.py:149
  114.1 31.9 %all-gather.16.cloned.1.call-done = bf16[2048,1024]{1,0:T(8,128)(2,1)} async-done(((bf16[128,1024]{1,0:T(8,128)(2,1)}), bf16[2048,1024]{1,0:T(8,128)(2,1)}) %all-gather.16.cloned.1.call-update) | async-done | bytes 4194320 | tf_op jit(solution)/shard_map/all_gather | solution.py:128
  212.9 31.3 %all-gather.2 = bf16[16,1,128]{2,1,0:T(2,128)(2,1)S(1)} all-gather(bf16[1,1,128]{2,1,0:T(2,128)(2,1)S(1)} %convert_bitcast_fusion.1), channel_id=1, replica_groups=mesh['dp'=4,'seq'=4,'tensor'=2] {'dp','seq'}, dimensions={0}, use_global_device_ids=true | all-gather | bytes 4352 | tf_op jit(solution)/shard_map/all_gather | solution.py:129
  244.2 22.5 %all-reduce.8.cloned.1.call-done = bf16[512,2048]{1,0:T(8,128)(2,1)} async-done(((bf16[512,2048]{1,0:T(8,128)(2,1)}), bf16[512,2048]{1,0:T(8,128)(2,1)}) %all-reduce.8.cloned.1.call-update) | async-done | bytes 2097168 | tf_op jit(solution)/shard_map/psum | solution.py:185
  271.6 124.2 %all-gather.22.cloned.1.call-done = bf16[2048,4096]{1,0:T(8,128)(2,1)} async-done(((bf16[128,4096]{1,0:T(8,128)(2,1)}), bf16[2048,4096]{1,0:T(8,128)(2,1)}) %all-gather.22.cloned.1.call-update) | async-done | bytes 16777232 | tf_op jit(solution)/shard_map/all_gather | solution.py:129
  395.8 15.1 fusion.159
  411.0 112.3 %all-gather.20.cloned.1.call-done = bf16[2048,4096]{1,0:T(8,128)(2,1)} async-done(((bf16[128,4096]{1,0:T(8,128)(2,1)}), bf16[2048,4096]{1,0:T(8,128)(2,1)}) %all-gather.20.cloned.1.call-update) | async-done | bytes 16777232 | tf_op jit(solution)/shard_map/all_gather | solution.py:129
  523.3 15.0 fusion.158
  538.3 112.4 %all-gather.24.cloned.1.call-done = bf16[2048,4096]{1,0:T(8,128)(2,1)} async-done(((bf16[128,4096]{1,0:T(8,128)(2,1)}), bf16[2048,4096]{1,0:T(8,128)(2,1)}) %all-gather.24.cloned.1.call-update) | async-done | bytes 16777232 | tf_op jit(solution)/shard_map/all_gather | solution.py:129
  650.7 22.2 %multiply_convert_fusion = (bf16[512,4096]{1,0:T(8,128)(2,1)}, bf16[512,4096]{1,0:T(8,128)(2,1)}, bf16[512,4096]{1,0:T(8,128)(2,1)}) fusion(f32[512,4096]{1,0:T(8,128)} %fusion.158, f32[512,4096]{1,0:T(8,128)} %fusion.159, bf16[512,2048]{1,0:T(8,128)(2,1)} %param.14, bf16[2048,4096]{1,0:T(8,128)(2,1)} %all-gather.24.cloned.1.call-done), kind=kOutput, calls=%fused_computation.43 | convolution fusion | flops 8621391872 | bytes 48234496 | tf_op jit(solution)/shard_map/dot_general | solution.py:200
  672.8 15.4 fusion.160
  702.7 15.5 convolution_convert_fusion.5
  718.2 39.4 %all-gather.26.cloned.1.call-done = bf16[1024,2048]{1,0:T(8,128)(2,1)} async-done(((bf16[512,2048]{1,0:T(8,128)(2,1)}), bf16[1024,2048]{1,0:T(8,128)(2,1)}) %all-gather.26.cloned.1.call-update) | async-done | bytes 4194320 | tf_op jit(solution)/shard_map/all_gather | solution.py:206
  922.6 21.0 %copy.109 = bf16[2048,4096]{1,0:T(8,128)(2,1)} copy(bf16[2048,4096]{0,1:T(8,128)(2,1)} %convert_bitcast_fusion) | data formatting | bytes 33554432
  977.4 18.7 %reduce-scatter.18.cloned.1.call-done = bf16[128,256]{1,0:T(8,128)(2,1)} async-done(((bf16[2048,256]{1,0:T(8,128)(2,1)}), bf16[128,256]{1,0:T(8,128)(2,1)}) %reduce-scatter.18.cloned.1.call-update) | async-done | bytes 65552 | tf_op jit(solution)/shard_map/reduce_scatter | solution.py:220
  997.7 108.9 %all-reduce.10.cloned.1.call-done = (bf16[512,2048]{1,0:T(8,128)(2,1)}, bf16[512,2048]{1,0:T(8,128)(2,1)}) async-done(((bf16[512,2048]{1,0:T(8,128)(2,1)}, bf16[512,2048]{1,0:T(8,128)(2,1)}), (bf16[512,2048]{1,0:T(8,128)(2,1)}, bf16[512,2048]{1,0:T(8,128)(2,1)})) %all-reduce.10.cloned.1.call-update) | async-done | bytes 4194320 | tf_op jit(solution)/shard_map/psum | solution.py:195
  1109.5 62.4 %all-reduce.3 = (f32[2048]{0:T(1024)S(1)}, f32[2048]{0:T(1024)S(1)}) all-reduce(f32[2048]{0:T(1024)S(1)} %get-tuple-element.46, f32[2048]{0:T(1024)S(1)} %copy-done.58), channel_id=5, replica_groups=mesh['dp'=4,'seq'=4,'tensor'=2] {'dp','seq'}, use_global_device_ids=true, to_apply=%region_23.24.clone | all-reduce | flops 4096 | bytes 32768
  1185.1 73.9 %reduce-scatter.16.cloned.1.call-done = bf16[128,1024]{1,0:T(8,128)(2,1)} async-done(((bf16[2048,1024]{1,0:T(8,128)(2,1)}), bf16[128,1024]{1,0:T(8,128)(2,1)}) %reduce-scatter.16.cloned.1.call-update) | async-done | bytes 262160 | tf_op jit(solution)/shard_map/reduce_scatter | solution.py:220
  1260.8 178.6 %reduce-scatter.28.cloned.1.call-done = bf16[128,4096]{1,0:T(8,128)(2,1)} async-done(((bf16[2048,4096]{1,0:T(8,128)(2,1)}), bf16[128,4096]{1,0:T(8,128)(2,1)}) %reduce-scatter.28.cloned.1.call-update) | async-done | bytes 1048592
  1442.7 177.2 %reduce-scatter.26.cloned.1.call-done = bf16[128,4096]{1,0:T(8,128)(2,1)} async-done(((bf16[2048,4096]{1,0:T(8,128)(2,1)}), bf16[128,4096]{1,0:T(8,128)(2,1)}) %reduce-scatter.26.cloned.1.call-update) | async-done | bytes 1048592 | tf_op jit(solution)/shard_map/reduce_scatter | solution.py:220
  1622.6 177.8 %reduce-scatter.24.cloned.1.call-done = bf16[128,4096]{1,0:T(8,128)(2,1)} async-done(((bf16[2048,4096]{1,0:T(8,128)(2,1)}), bf16[128,4096]{1,0:T(8,128)(2,1)}) %reduce-scatter.24.cloned.1.call-update) | async-done | bytes 1048592 | tf_op jit(solution)/shard_map/reduce_scatter | solution.py:220
  (350 shorter events, 333.5 us)
Async XLA Ops:
  7.2 48.1 %all-gather.12.cloned.1.call-start = ((), (), s32[]{:S(2)}) async-start(), calls=%async_computation.9 | async-start | bytes 1114112 | tf_op jit(solution)/shard_map/all_gather | solution.py:128
  9.0 82.9 %all-gather.14.cloned.1.call-start = ((), (), s32[]{:S(2)}) async-start(), calls=%async_computation.10 | async-start | bytes 1114112 | tf_op jit(solution)/shard_map/all_gather | solution.py:128
  10.6 135.3 %all-gather.16.cloned.1.call-start = ((), (), s32[]{:S(2)}) async-start(), calls=%async_computation.11 | async-start | bytes 4456448 | tf_op jit(solution)/shard_map/all_gather | solution.py:128
  12.4 185.8 %all-gather.18.cloned.1.call-start = ((), (), s32[]{:S(2)}) async-start(), calls=%async_computation.12 | async-start | bytes 4456448 | tf_op jit(solution)/shard_map/all_gather | solution.py:128
  14.3 252.4 %all-reduce.8.cloned.1.call-start = ((), (), s32[]{:S(2)}) async-start(), calls=%async_computation.13 | async-start | bytes 4194304 | tf_op jit(solution)/shard_map/psum | solution.py:185
  18.5 127.4 %copy-start.59 = (f32[512]{0:T(512)}, f32[512]{0:T(512)S(1)}, u32[]{:S(2)}) copy-start(f32[512]{0:T(512)S(1)} %add_rsqrt_fusion.1) | copy-start | bytes 6148
  52.4 93.5 %copy-start.50 = (f32[16,1,128]{2,1,0:T(1,128)}, f32[16,1,128]{2,1,0:T(1,128)S(1)}, u32[]{:S(2)}) copy-start(f32[16,1,128]{2,1,0:T(1,128)S(1)} %convert_element_type.285) | copy-start | bytes 24580
  54.0 96.8 %copy-start.16 = (f32[512,64]{0,1:T(8,128)}, f32[512,64]{0,1:T(8,128)S(1)}, u32[]{:S(2)}) copy-start(f32[512,64]{0,1:T(8,128)S(1)} %get-tuple-element.70) | copy-start | bytes 393220
  94.3 73.3 %copy-start.11 = (bf16[256,4,64]{0,2,1:T(8,128)(2,1)}, bf16[256,4,64]{0,2,1:T(8,128)(2,1)S(1)}, u32[]{:S(2)}) copy-start(bf16[256,4,64]{0,2,1:T(8,128)(2,1)S(1)} %get-tuple-element.68) | copy-start | bytes 393220
  204.5 191.3 %all-gather.22.cloned.1.call-start = ((), (), s32[]{:S(2)}) async-start(), calls=%async_computation.15 | async-start | bytes 17825792 | tf_op jit(solution)/shard_map/all_gather | solution.py:129
  207.3 315.9 %all-gather.20.cloned.1.call-start = ((), (), s32[]{:S(2)}) async-start(), calls=%async_computation.14 | async-start | bytes 17825792 | tf_op jit(solution)/shard_map/all_gather | solution.py:129
  210.1 440.6 %all-gather.24.cloned.1.call-start = ((), (), s32[]{:S(2)}) async-start(), calls=%async_computation.16 | async-start | bytes 17825792 | tf_op jit(solution)/shard_map/all_gather | solution.py:129
  212.8 544.7 %all-gather.26.cloned.1.call-start = ((), (), s32[]{:S(2)}) async-start(), calls=%async_computation.25 | async-start | bytes 6291456 | tf_op jit(solution)/shard_map/all_gather | solution.py:206
  702.5 160.7 %reduce-scatter.14.cloned.1.call-start = ((), (), s32[]{:S(2)}) async-start(), calls=%async_computation.18 | async-start | bytes 655360 | tf_op jit(solution)/shard_map/reduce_scatter | solution.py:270
  810.5 65.9 %reduce-scatter.12.cloned.1.call-start = ((), (), s32[]{:S(2)}) async-start(), calls=%async_computation.17 | async-start | bytes 655360 | tf_op jit(solution)/shard_map/reduce_scatter | solution.py:267
  854.5 121.5 %reduce-scatter.20.cloned.1.call-start = ((), (), s32[]{:S(2)}) async-start(), calls=%async_computation.21 | async-start | bytes 1114112 | tf_op jit(solution)/shard_map/reduce_scatter | solution.py:220
  866.4 129.8 %reduce-scatter.18.cloned.1.call-start = ((), (), s32[]{:S(2)}) async-start(), calls=%async_computation.20 | async-start | bytes 1114112 | tf_op jit(solution)/shard_map/reduce_scatter | solution.py:220
  882.2 224.4 %all-reduce.10.cloned.1.call-start = ((), (), s32[]{:S(2)}) async-start(), calls=%async_computation.27 | async-start | bytes 8388608 | tf_op jit(solution)/shard_map/psum | solution.py:195
  891.7 291.6 %reduce-scatter.22.cloned.1.call-start = ((), (), s32[]{:S(2)}) async-start(), calls=%async_computation.22 | async-start | bytes 4456448 | tf_op jit(solution)/shard_map/reduce_scatter | solution.py:220
  901.7 357.2 %reduce-scatter.16.cloned.1.call-start = ((), (), s32[]{:S(2)}) async-start(), calls=%async_computation.19 | async-start | bytes 4456448 | tf_op jit(solution)/shard_map/reduce_scatter | solution.py:220
  907.6 531.9 %reduce-scatter.28.cloned.1.call-start = ((), (), s32[]{:S(2)}) async-start(), calls=%async_computation.26 | async-start | bytes 17825792
  943.6 676.2 %reduce-scatter.26.cloned.1.call-start = ((), (), s32[]{:S(2)}) async-start(), calls=%async_computation.24 | async-start | bytes 17825792 | tf_op jit(solution)/shard_map/reduce_scatter | solution.py:220
  958.7 841.7 %reduce-scatter.24.cloned.1.call-start = ((), (), s32[]{:S(2)}) async-start(), calls=%async_computation.23 | async-start | bytes 17825792 | tf_op jit(solution)/shard_map/reduce_scatter | solution.py:220
  974.0 135.5 %copy-start.58 = (f32[2048]{0:T(1024)S(1)}, f32[2048]{0:T(1024)}, u32[]{:S(2)}) copy-start(f32[2048]{0:T(1024)} %get-tuple-element.44) | copy-start | bytes 24580
  (82 other events, 886.4 us)
Sparse Core Ops, SparseCore 0:
  10.8 40.5 all-gather.11
  54.2 37.6 all-gather.13
  94.7 51.2 all-gather.15
  148.6 48.9 all-gather.17
  204.7 62.0 all-reduce.7
  269.4 126.4 all-gather.21
  398.6 124.5 all-gather.19
  526.0 124.5 all-gather.23
  702.7 54.8 all-gather.25
  810.7 21.8 reduce-scatter.13
  854.6 21.8 reduce-scatter.11
  879.9 55.9 reduce-scatter.19
  939.5 56.6 reduce-scatter.17
  999.7 106.8 all-reduce.9
  1110.3 72.9 reduce-scatter.21
  1187.0 71.8 reduce-scatter.15
  1262.9 176.4 reduce-scatter.27
  1443.4 176.4 reduce-scatter.25
  1624.0 176.4 reduce-scatter.23
